TPU v7x, 256 devices: a whole 4x4x8 slice. The times are simulated.
256 devices in a mesh: ex: 16 (over y_hi, x, core), co: 16 (over y_lo, z).
Axes of the slice: x: 4, y: 4 (y_hi: 2, y_lo: 2; y = y_hi * 2 + y_lo), z: 8, core: 2. Of those that a mesh axis runs over, the one named last changes fastest.
Arguments:
- train_grads: float32 [16384, 32768], P('ex', 'co')
- queries: float32 [1024, 32768], P('ex', 'co'), may hold values from -6 to 6
- module_ids: int32 [8], replicated, may hold values from 0 to 223
- module_scale: float32 [224], replicated, may hold values from 0.3 to 3
- example_ids: int32 [16384], P('ex'), may hold values from 0 to 16383, as said below
Outputs:
- influence: float32 [1024, 16384], P('co', 'ex')
Inputs may be any that keep to these rules, and one draw needn't show every extreme that they name: `example_ids`: the examples of block s of 1024 rows carry the ids s * 1024 to (s + 1) * 1024 - 1, each once.
All inputs are finite; a program needn't handle non-finite values.
Results may differ from a plain program's by a relative error of at most 0.00008.
Values sent between devices are 32-bit elements; how exact they have to be, the bound alone decides.
No kernel may reach another device: no remote copies, remote signals or barrier semaphores. Data moves between devices by JAX's collectives and lax.ppermute only.
A program may use at most 128 MiB of HBM per device.

v0:
```python
import jax
import jax.numpy as jnp
from jax import lax
from jax.sharding import PartitionSpec as P

PROJ = 4096
CHUNKS = 4
epsilon = 1e-06


def shards(train_grads, queries, module_ids, module_scale, example_ids):
    example_count, coord_count = train_grads.shape
    offset = lax.axis_index("co") * coord_count
    position = offset + lax.iota(jnp.int32, coord_count)
    table_index = lax.iota(jnp.int32, module_scale.shape[0])
    picked = jnp.sum(
        jnp.where(module_ids[:, None] == table_index[None, :], module_scale[None, :], 0.0), axis=1
    )
    window_index = lax.iota(jnp.int32, module_ids.shape[0])
    coord_scale = jnp.sum(
        jnp.where((position // PROJ)[:, None] == window_index[None, :], picked[None, :], 0.0),
        axis=1,
    )
    scaled = queries * coord_scale[None, :]
    squares = jnp.sum(train_grads * train_grads, axis=1)
    norm_total = lax.all_gather(squares, "co").sum(0)
    inverse_norm = lax.rsqrt(norm_total + epsilon)
    rows = queries.shape[0] // CHUNKS
    outs = []
    for k in range(CHUNKS):
        all_q = lax.all_gather(scaled[k * rows : (k + 1) * rows], "ex", axis=0, tiled=True)
        s = lax.dot_general(
            all_q,
            train_grads,
            (((1,), (1,)), ((), ())),
            precision=lax.Precision.HIGH,
            preferred_element_type=jnp.float32,
        )
        outs.append(lax.psum_scatter(s, "co", scatter_dimension=0, tiled=True))
    own = jnp.concatenate(outs, 0)
    normed = own * inverse_norm[None, :]
    local_ids = example_ids - lax.axis_index("ex") * example_count
    return jnp.zeros_like(normed).at[:, local_ids].set(normed)


def solution(mesh):
    return jax.shard_map(
        shards,
        mesh=mesh,
        in_specs=(P("ex", "co"), P("ex", "co"), P(), P(), P("ex")),
        out_specs=P("co", "ex"),
        check_vma=False,
    )
```

profile of v0, /device:TPU:2, one launch (start us, length us, event | category | flops | bytes accessed | tf_op | source)
XLA Modules:
  0.0 527.2 jit_solution(14822634921270370738)
XLA Ops:
  6.5 0.0 all-gather.12.cloned.1.call-start
  6.6 0.9 select_reduce_fusion.1
  7.4 0.1 select_reduce_fusion
  7.5 1.1 broadcast_multiply_fusion
  8.6 0.8 fusion.6
  9.4 0.0 all-gather.12.cloned.1.call-update
  9.4 0.0 all-gather.6.cloned.1.call-start
  9.5 0.7 all-gather.6.cloned.1.call-update
  10.2 0.0 all-gather.8.cloned.1.call-start
  10.2 0.7 all-gather.8.cloned.1.call-update
  10.9 0.0 all-gather.10.cloned.1.call-start
  11.0 0.5 all-gather.10.cloned.1.call-update
  11.5 0.0 reduce-scatter.11.cloned.1.call-start
  11.5 54.8 %all-gather.12.cloned.1.call-done = f32[256,2048]{1,0:T(8,128)} async-done(((f32[16,2048]{1,0:T(8,128)}), f32[256,2048]{1,0:T(8,128)}) %all-gather.12.cloned.1.call-update) | async-done | bytes 2097168 | tf_op jit(solution)/shard_map/all_gather | solution.py:31
  66.3 8.7 %fusion.10 = f32[256,1024]{1,0:T(8,128)} fusion(f32[256,2048]{1,0:T(8,128)} %all-gather.12.cloned.1.call-done, f32[1024,2048]{1,0:T(8,128)} %param.5), kind=kOutput, calls=%fused_computation.26 | convolution fusion | flops 3221225472 | bytes 11534336 | tf_op jit(solution)/shard_map/dot_general | solution.py:32
  75.0 0.0 reduce-scatter.11.cloned.1.call-update
  75.0 0.0 reduce-scatter.5.cloned.1.call-start
  75.1 46.4 %all-gather.6.cloned.1.call-done = f32[256,2048]{1,0:T(8,128)} async-done(((f32[16,2048]{1,0:T(8,128)}), f32[256,2048]{1,0:T(8,128)}) %all-gather.6.cloned.1.call-update) | async-done | bytes 2097168 | tf_op jit(solution)/shard_map/all_gather | solution.py:31
  121.5 8.6 %fusion.7 = f32[256,1024]{1,0:T(8,128)} fusion(f32[256,2048]{1,0:T(8,128)} %all-gather.6.cloned.1.call-done, f32[1024,2048]{1,0:T(8,128)} %param.5), kind=kOutput, calls=%fused_computation.23 | convolution fusion | flops 3221225472 | bytes 11534336 | tf_op jit(solution)/shard_map/dot_general | solution.py:32
  130.1 0.0 reduce-scatter.5.cloned.1.call-update
  130.1 0.0 reduce-scatter.7.cloned.1.call-start
  130.2 46.5 %all-gather.8.cloned.1.call-done = f32[256,2048]{1,0:T(8,128)} async-done(((f32[16,2048]{1,0:T(8,128)}), f32[256,2048]{1,0:T(8,128)}) %all-gather.8.cloned.1.call-update) | async-done | bytes 2097168 | tf_op jit(solution)/shard_map/all_gather | solution.py:31
  176.6 8.6 %fusion.8 = f32[256,1024]{1,0:T(8,128)} fusion(f32[256,2048]{1,0:T(8,128)} %all-gather.8.cloned.1.call-done, f32[1024,2048]{1,0:T(8,128)} %param.5), kind=kOutput, calls=%fused_computation.24 | convolution fusion | flops 3221225472 | bytes 11534336 | tf_op jit(solution)/shard_map/dot_general | solution.py:32
  185.2 0.0 reduce-scatter.7.cloned.1.call-update
  185.3 0.2 reduce-scatter.9.cloned.1.call-start
  185.5 46.1 %all-gather.10.cloned.1.call-done = f32[256,2048]{1,0:T(8,128)} async-done(((f32[16,2048]{1,0:T(8,128)}), f32[256,2048]{1,0:T(8,128)}) %all-gather.10.cloned.1.call-update) | async-done | bytes 2097168 | tf_op jit(solution)/shard_map/all_gather | solution.py:31
  231.6 8.6 %fusion.9 = f32[256,1024]{1,0:T(8,128)} fusion(f32[256,2048]{1,0:T(8,128)} %all-gather.10.cloned.1.call-done, f32[1024,2048]{1,0:T(8,128)} %param.5), kind=kOutput, calls=%fused_computation.25 | convolution fusion | flops 3221225472 | bytes 11534336 | tf_op jit(solution)/shard_map/dot_general | solution.py:32
  240.2 0.0 reduce-scatter.9.cloned.1.call-update
  240.3 0.0 copy-start
  240.3 4.0 multiply_reduce_fusion
  244.3 33.3 %all-gather = f32[16384]{0:T(1024)S(1)} all-gather(f32[1024]{0:T(1024)S(1)} %multiply_reduce_fusion), channel_id=2, replica_groups=mesh['ex'=16,'co'=16] {'co'}, dimensions={0}, use_global_device_ids=true | all-gather | bytes 69632 | tf_op jit(solution)/shard_map/all_gather | solution.py:26
  277.6 0.0 copy-done
  277.7 27.0 %reduce-scatter.11.cloned.1.call-done = f32[16,1024]{1,0:T(8,128)} async-done(((f32[256,1024]{1,0:T(8,128)}), f32[16,1024]{1,0:T(8,128)}) %reduce-scatter.11.cloned.1.call-update) | async-done | bytes 65552 | tf_op jit(solution)/shard_map/reduce_scatter | solution.py:39
  304.6 70.1 %reduce-scatter.5.cloned.1.call-done = f32[16,1024]{1,0:T(8,128)} async-done(((f32[256,1024]{1,0:T(8,128)}), f32[16,1024]{1,0:T(8,128)}) %reduce-scatter.5.cloned.1.call-update) | async-done | bytes 65552 | tf_op jit(solution)/shard_map/reduce_scatter | solution.py:39
  374.8 70.1 %reduce-scatter.7.cloned.1.call-done = f32[16,1024]{1,0:T(8,128)} async-done(((f32[256,1024]{1,0:T(8,128)}), f32[16,1024]{1,0:T(8,128)}) %reduce-scatter.7.cloned.1.call-update) | async-done | bytes 65552 | tf_op jit(solution)/shard_map/reduce_scatter | solution.py:39
  444.8 70.2 %reduce-scatter.9.cloned.1.call-done = f32[16,1024]{1,0:T(8,128)} async-done(((f32[256,1024]{1,0:T(8,128)}), f32[16,1024]{1,0:T(8,128)}) %reduce-scatter.9.cloned.1.call-update) | async-done | bytes 65552 | tf_op jit(solution)/shard_map/reduce_scatter | solution.py:39
  515.1 1.0 fusion
  516.0 0.2 copy.10
  516.2 3.2 scatter_custom_fusion
  519.5 0.9 copy.11
  (5 shorter events, 0.1 us)
Async XLA Ops:
  6.5 59.8 %all-gather.12.cloned.1.call-start = ((), (), s32[]{:S(2)}) async-start(), calls=%async_computation.10 | async-start | bytes 2228224 | tf_op jit(solution)/shard_map/all_gather | solution.py:31
  9.4 112.0 %all-gather.6.cloned.1.call-start = ((), (), s32[]{:S(2)}) async-start(), calls=%async_computation.4 | async-start | bytes 2228224 | tf_op jit(solution)/shard_map/all_gather | solution.py:31
  10.2 166.5 %all-gather.8.cloned.1.call-start = ((), (), s32[]{:S(2)}) async-start(), calls=%async_computation.6 | async-start | bytes 2228224 | tf_op jit(solution)/shard_map/all_gather | solution.py:31
  10.9 220.7 %all-gather.10.cloned.1.call-start = ((), (), s32[]{:S(2)}) async-start(), calls=%async_computation.8 | async-start | bytes 2228224 | tf_op jit(solution)/shard_map/all_gather | solution.py:31
  11.5 293.1 %reduce-scatter.11.cloned.1.call-start = ((), (), s32[]{:S(2)}) async-start(), calls=%async_computation.11 | async-start | bytes 1114112 | tf_op jit(solution)/shard_map/reduce_scatter | solution.py:39
  75.0 299.7 %reduce-scatter.5.cloned.1.call-start = ((), (), s32[]{:S(2)}) async-start(), calls=%async_computation.5 | async-start | bytes 1114112 | tf_op jit(solution)/shard_map/reduce_scatter | solution.py:39
  130.1 314.7 %reduce-scatter.7.cloned.1.call-start = ((), (), s32[]{:S(2)}) async-start(), calls=%async_computation.7 | async-start | bytes 1114112 | tf_op jit(solution)/shard_map/reduce_scatter | solution.py:39
  185.3 329.8 %reduce-scatter.9.cloned.1.call-start = ((), (), s32[]{:S(2)}) async-start(), calls=%async_computation.9 | async-start | bytes 1114112 | tf_op jit(solution)/shard_map/reduce_scatter | solution.py:39
  240.3 37.4 %copy-start = (s32[1024]{0:T(1024)S(1)}, s32[1024]{0:T(1024)}, u32[]{:S(2)}) copy-start(s32[1024]{0:T(1024)} %param.9) | copy-start | bytes 12292
Sparse Core Ops, SparseCore 0:
  10.1 56.1 all-gather.11
  69.1 52.3 all-gather.5
  124.2 52.3 all-gather.7
  179.2 52.3 all-gather.9
  234.0 70.5 reduce-scatter.10
  307.1 67.5 reduce-scatter.4
  377.3 67.5 reduce-scatter.6
  447.5 67.5 reduce-scatter.8
where the time goes:
time: 527 us
  waiting for transfers between devices  433 us (82%)
  matrix products  34.5 us (7%)
  blocking collectives  33.3 us (6%)
  between operations  13.6 us (3%)
  other arithmetic  7.04 us (1%)
    reduce_scatter x4, waiting for transfers between devices, shards(): outs.append(lax.psum_scatter(s, 'co', scatter_dimension=0, tiled=True))  237 us
    all_gather x4, waiting for transfers between devices, shards(): lax.all_gather(scaled[k * rows:(k + 1) * rows], 'ex', axis=0, tiled=True)  194 us
    dot_general x4, matrix products, shards(): lax.dot_general(all_q, train_grads, (((1,), (1,)), ((), ())), precision=l...  34.5 us
    all_gather x1, blocking collectives, shards(): norm_total = lax.all_gather(squares, 'co').sum(0)  33.3 us
  transfers between devices with their start and end apart: 8, of which 8 were waited for; matrix products, arithmetic and copies ran while one was open for 7% of the time, Pallas kernels for 0%

commit v1 on v0

--- a/solution.py
+++ b/solution.py
@@ -1,3 +1,4 @@
+import functools
 import jax
 import jax.numpy as jnp
 from jax import lax
@@ -6,6 +7,15 @@
 PROJ = 4096
 CHUNKS = 4
 epsilon = 1e-06
+
+
+def detail_vector(inputs, in_dim):
+    return jnp.concatenate(
+        lax.all_to_all(jnp.stack([inputs] * lax.axis_size("ex"), 0), "ex", 0, 0), axis=in_dim
+    )
+
+
+watch_keys_on_mesh = functools.partial(detail_vector, in_dim=0)
 
 
 def shards(train_grads, queries, module_ids, module_scale, example_ids):
@@ -28,7 +38,7 @@
     rows = queries.shape[0] // CHUNKS
     outs = []
     for k in range(CHUNKS):
-        all_q = lax.all_gather(scaled[k * rows : (k + 1) * rows], "ex", axis=0, tiled=True)
+        all_q = watch_keys_on_mesh(scaled[k * rows : (k + 1) * rows])
         s = lax.dot_general(
             all_q,
             train_grads,

time: 527 us -> 365 us (0.69)
  waiting for transfers between devices: 433 us -> 214 us
  blocking collectives: 33.3 us -> 68.9 us
  starting transfers between devices: 0.46 us -> 19 us
    all_gather x4 -> x0, waiting for transfers between devices: 194 us -> none  [shards(): lax.all_gather(scaled[k * rows:(k + 1) * rows], 'ex', axis=0, tiled=True)]
    reduce_scatter x4, waiting for transfers between devices: 237 us -> 150 us  [shards(): outs.append(lax.psum_scatter(s, 'co', scatter_dimension=0, tiled=True))]
    all_to_all x0 -> x3, waiting for transfers between devices: none -> 64.1 us  [detail_vector(): lax.all_to_all(jnp.stack([inputs] * lax.axis_size('ex'), 0), 'ex', 0, 0)]
    all_to_all x0 -> x1, blocking collectives: none -> 33 us  [detail_vector(): lax.all_to_all(jnp.stack([inputs] * lax.axis_size('ex'), 0), 'ex', 0, 0)]
    all_to_all x0 -> x3, starting transfers between devices: none -> 18.6 us  [detail_vector(): lax.all_to_all(jnp.stack([inputs] * lax.axis_size('ex'), 0), 'ex', 0, 0)]
  transfers between devices with their start and end apart: 8 -> 7, of which waited for: 8 -> 6; matrix products, arithmetic and copies ran while one was open for 7% -> 11% of each run, Pallas kernels for 0% -> 0%
where the time goes in v1:
time: 365 us
  waiting for transfers between devices  214 us (59%)
  blocking collectives  68.9 us (19%)
  matrix products  32.9 us (9%)
  starting transfers between devices  19 us (5%)
  between operations  13.2 us (4%)
  local copies, waits for them, and re-layouts  9.69 us (3%)
  other arithmetic  7.04 us (2%)
    reduce_scatter x4, waiting for transfers between devices, shards(): outs.append(lax.psum_scatter(s, 'co', scatter_dimension=0, tiled=True))  150 us
    all_to_all x3, waiting for transfers between devices, detail_vector(): lax.all_to_all(jnp.stack([inputs] * lax.axis_size('ex'), 0), 'ex', 0, 0)  64.1 us
    all_gather x1, blocking collectives, shards(): norm_total = lax.all_gather(squares, 'co').sum(0)  35.9 us
    all_to_all x1, blocking collectives, detail_vector(): lax.all_to_all(jnp.stack([inputs] * lax.axis_size('ex'), 0), 'ex', 0, 0)  33 us
    dot_general x4, matrix products, shards(): lax.dot_general(all_q, train_grads, (((1,), (1,)), ((), ())), precision=l...  32.9 us
    all_to_all x3, starting transfers between devices, detail_vector(): lax.all_to_all(jnp.stack([inputs] * lax.axis_size('ex'), 0), 'ex', 0, 0)  18.6 us
  transfers between devices with their start and end apart: 7, of which 6 were waited for; matrix products, arithmetic and copies ran while one was open for 11% of the time, Pallas kernels for 0%

profile of v1, /device:TPU:2, one launch (start us, length us, event | category | flops | bytes accessed | tf_op | source)
XLA Modules:
  0.0 364.7 jit_solution(12885031734569632190)
XLA Ops:
  6.5 0.9 select_reduce_fusion.1
  7.4 0.1 select_reduce_fusion
  7.5 1.1 broadcast_multiply_fusion
  8.6 0.2 stack.11
  8.9 33.0 %all_to_all.20 = f32[16,16,2048]{2,1,0:T(8,128)} all-to-all(f32[16,16,2048]{2,1,0:T(8,128)S(1)} %stack.11), channel_id=1, replica_groups=mesh['ex'=16,'co'=16] {'ex'}, dimensions={0} | all-to-all | bytes 4194304 | tf_op jit(solution)/shard_map/all_to_all | solution.py:14
  41.8 1.6 stack.8
  43.4 7.2 %all-to-all-start = ((f32[16,16,2048]{2,1,0:T(8,128)}), f32[16,16,2048]{2,1,0:T(8,128)S(1)}, u32[]{:S(2)}, u32[]{:S(2)}) async-start(f32[16,16,2048]{2,1,0:T(8,128)} %stack.8), calls=%async_computation | async-start | bytes 4194304 | tf_op jit(solution)/shard_map/all_to_all | solution.py:14
  50.7 0.0 reduce-scatter.11.cloned.1.call-start
  50.7 8.6 %fusion.10 = f32[256,1024]{1,0:T(8,128)} fusion(f32[256,2048]{1,0:T(8,128)} %bitcast.16, f32[1024,2048]{1,0:T(8,128)} %param.5), kind=kOutput, calls=%fused_computation.26 | convolution fusion | flops 3221225472 | bytes 11534336 | tf_op jit(solution)/shard_map/dot_general | solution.py:42
  59.3 0.0 reduce-scatter.11.cloned.1.call-update
  59.3 19.9 %all-to-all-done = f32[16,16,2048]{2,1,0:T(8,128)S(1)} async-done(((f32[16,16,2048]{2,1,0:T(8,128)}), f32[16,16,2048]{2,1,0:T(8,128)S(1)}, u32[]{:S(2)}, u32[]{:S(2)}) %all-to-all-start) | async-done | bytes 2097184 | tf_op jit(solution)/shard_map/all_to_all | solution.py:14
  79.2 0.0 copy-start
  79.2 1.7 stack.9
  81.0 0.2 copy-done
  81.2 5.6 %all-to-all-start.1 = ((f32[16,16,2048]{2,1,0:T(8,128)}), f32[16,16,2048]{2,1,0:T(8,128)S(1)}, u32[]{:S(2)}, u32[]{:S(2)}) async-start(f32[16,16,2048]{2,1,0:T(8,128)} %stack.9), calls=%async_computation.2 | async-start | bytes 4194304 | tf_op jit(solution)/shard_map/all_to_all | solution.py:14
  86.8 0.0 reduce-scatter.5.cloned.1.call-start
  86.9 8.7 %fusion.7 = f32[256,1024]{1,0:T(8,128)} fusion(f32[256,2048]{1,0:T(8,128)} %bitcast.15, f32[1024,2048]{1,0:T(8,128)} %param.5), kind=kOutput, calls=%fused_computation.23 | convolution fusion | flops 3221225472 | bytes 11534336 | tf_op jit(solution)/shard_map/dot_general | solution.py:42
  95.5 0.0 reduce-scatter.5.cloned.1.call-update
  95.6 22.2 %all-to-all-done.1 = f32[16,16,2048]{2,1,0:T(8,128)S(1)} async-done(((f32[16,16,2048]{2,1,0:T(8,128)}), f32[16,16,2048]{2,1,0:T(8,128)S(1)}, u32[]{:S(2)}, u32[]{:S(2)}) %all-to-all-start.1) | async-done | bytes 2097184 | tf_op jit(solution)/shard_map/all_to_all | solution.py:14
  117.8 1.5 stack.10
  119.3 5.8 %all-to-all-start.2 = ((f32[16,16,2048]{2,1,0:T(8,128)}), f32[16,16,2048]{2,1,0:T(8,128)}, u32[]{:S(2)}, u32[]{:S(2)}) async-start(f32[16,16,2048]{2,1,0:T(8,128)} %stack.10), calls=%async_computation.4 | async-start | bytes 4194304 | tf_op jit(solution)/shard_map/all_to_all | solution.py:14
  125.1 0.0 reduce-scatter.7.cloned.1.call-start
  125.1 7.0 %fusion.8 = f32[256,1024]{1,0:T(8,128)} fusion(f32[256,2048]{1,0:T(8,128)S(1)} %bitcast.14, f32[1024,2048]{1,0:T(8,128)} %param.5), kind=kOutput, calls=%fused_computation.24 | convolution fusion | flops 3221225472 | bytes 11534336 | tf_op jit(solution)/shard_map/dot_general | solution.py:42
  132.2 0.0 reduce-scatter.7.cloned.1.call-update
  132.2 0.2 reduce-scatter.9.cloned.1.call-start
  132.4 22.0 %all-to-all-done.2 = f32[16,16,2048]{2,1,0:T(8,128)} async-done(((f32[16,16,2048]{2,1,0:T(8,128)}), f32[16,16,2048]{2,1,0:T(8,128)}, u32[]{:S(2)}, u32[]{:S(2)}) %all-to-all-start.2) | async-done | bytes 2097184 | tf_op jit(solution)/shard_map/all_to_all | solution.py:14
  154.4 8.6 %fusion.9 = f32[256,1024]{1,0:T(8,128)} fusion(f32[256,2048]{1,0:T(8,128)} %bitcast.2, f32[1024,2048]{1,0:T(8,128)} %param.5), kind=kOutput, calls=%fused_computation.25 | convolution fusion | flops 3221225472 | bytes 11534336 | tf_op jit(solution)/shard_map/dot_general | solution.py:42
  163.0 0.0 reduce-scatter.9.cloned.1.call-update
  163.0 0.0 copy-start.1
  163.0 4.0 %multiply_reduce_fusion = f32[1024]{0:T(1024)S(1)} fusion(f32[1024,2048]{1,0:T(8,128)} %param.5), kind=kLoop, calls=%fused_computation.1 | loop fusion | flops 4193280 | bytes 8392704 | tf_op jit(solution)/shard_map/reduce_sum | solution.py:35
  167.0 35.9 %all-gather = f32[16384]{0:T(1024)S(1)} all-gather(f32[1024]{0:T(1024)S(1)} %multiply_reduce_fusion), channel_id=2, replica_groups=mesh['ex'=16,'co'=16] {'co'}, dimensions={0}, use_global_device_ids=true | all-gather | bytes 69632 | tf_op jit(solution)/shard_map/all_gather | solution.py:36
  203.0 0.0 copy-done.1
  203.1 0.0 reduce-scatter.11.cloned.1.call-done
  203.1 9.6 %reduce-scatter.5.cloned.1.call-done = f32[16,1024]{1,0:T(8,128)} async-done(((f32[256,1024]{1,0:T(8,128)}), f32[16,1024]{1,0:T(8,128)}) %reduce-scatter.5.cloned.1.call-update) | async-done | bytes 65552 | tf_op jit(solution)/shard_map/reduce_scatter | solution.py:49
  212.7 70.1 %reduce-scatter.7.cloned.1.call-done = f32[16,1024]{1,0:T(8,128)} async-done(((f32[256,1024]{1,0:T(8,128)}), f32[16,1024]{1,0:T(8,128)}) %reduce-scatter.7.cloned.1.call-update) | async-done | bytes 65552 | tf_op jit(solution)/shard_map/reduce_scatter | solution.py:49
  282.8 70.1 %reduce-scatter.9.cloned.1.call-done = f32[16,1024]{1,0:T(8,128)} async-done(((f32[256,1024]{1,0:T(8,128)}), f32[16,1024]{1,0:T(8,128)}) %reduce-scatter.9.cloned.1.call-update) | async-done | bytes 65552 | tf_op jit(solution)/shard_map/reduce_scatter | solution.py:49
  352.9 1.0 fusion
  353.8 0.2 copy.10
  354.0 3.2 scatter_custom_fusion
  357.3 0.9 copy.11
  (6 shorter events, 0.1 us)
Async XLA Ops:
  43.4 35.8 %all-to-all-start = ((f32[16,16,2048]{2,1,0:T(8,128)}), f32[16,16,2048]{2,1,0:T(8,128)S(1)}, u32[]{:S(2)}, u32[]{:S(2)}) async-start(f32[16,16,2048]{2,1,0:T(8,128)} %stack.8), calls=%async_computation | async-start | bytes 4194304 | tf_op jit(solution)/shard_map/all_to_all | solution.py:14
  50.7 152.4 %reduce-scatter.11.cloned.1.call-start = ((), (), s32[]{:S(2)}) async-start(), calls=%async_computation.11 | async-start | bytes 1114112 | tf_op jit(solution)/shard_map/reduce_scatter | solution.py:49
  79.2 2.0 copy-start
  81.2 36.6 %all-to-all-start.1 = ((f32[16,16,2048]{2,1,0:T(8,128)}), f32[16,16,2048]{2,1,0:T(8,128)S(1)}, u32[]{:S(2)}, u32[]{:S(2)}) async-start(f32[16,16,2048]{2,1,0:T(8,128)} %stack.9), calls=%async_computation.2 | async-start | bytes 4194304 | tf_op jit(solution)/shard_map/all_to_all | solution.py:14
  86.8 125.9 %reduce-scatter.5.cloned.1.call-start = ((), (), s32[]{:S(2)}) async-start(), calls=%async_computation.8 | async-start | bytes 1114112 | tf_op jit(solution)/shard_map/reduce_scatter | solution.py:49
  119.3 35.1 %all-to-all-start.2 = ((f32[16,16,2048]{2,1,0:T(8,128)}), f32[16,16,2048]{2,1,0:T(8,128)}, u32[]{:S(2)}, u32[]{:S(2)}) async-start(f32[16,16,2048]{2,1,0:T(8,128)} %stack.10), calls=%async_computation.4 | async-start | bytes 4194304 | tf_op jit(solution)/shard_map/all_to_all | solution.py:14
  125.1 157.7 %reduce-scatter.7.cloned.1.call-start = ((), (), s32[]{:S(2)}) async-start(), calls=%async_computation.9 | async-start | bytes 1114112 | tf_op jit(solution)/shard_map/reduce_scatter | solution.py:49
  132.2 220.7 %reduce-scatter.9.cloned.1.call-start = ((), (), s32[]{:S(2)}) async-start(), calls=%async_computation.10 | async-start | bytes 1114112 | tf_op jit(solution)/shard_map/reduce_scatter | solution.py:49
  163.0 40.0 %copy-start.1 = (s32[1024]{0:T(1024)S(1)}, s32[1024]{0:T(1024)}, u32[]{:S(2)}) copy-start(s32[1024]{0:T(1024)} %param.9) | copy-start | bytes 12292
Sparse Core Ops, SparseCore 0:
  59.5 84.6 reduce-scatter.10
  146.8 65.8 reduce-scatter.4
  215.2 67.5 reduce-scatter.6
  285.3 67.4 reduce-scatter.8
